TPU v7x, 512 devices: a whole 4x4x16 slice. The times are simulated.
512 devices in a mesh: clips: 32 (over y, x, core), slab: 16 (over z).
Axes of the slice: x: 4, y: 4, z: 16, core: 2. Of those that a mesh axis runs over, the one named last changes fastest.
Arguments:
- video: bfloat16 [64, 6, 16, 16, 256], P('clips', None, 'slab'), may hold values from -6 to 6
- clip_blocks: int32 [64], replicated, may hold values from 1 to 3, 128 in all
- deal_order: int32 [32], replicated, may hold values from 0 to 31, each once
- kernel: bfloat16 [256, 3456], P('clips', 'slab'), may hold values from -0.078125 to 0.078125
- gain: float32 [128], replicated, may hold values from 0.25 to 1.75
- bias: float32 [128], replicated, may hold values from -3 to 3
- cotangent: bfloat16 [128, 2, 16, 16, 128], P('clips', None, 'slab'), may hold values from -6 to 6
Outputs:
- activations: bfloat16 [128, 2, 16, 16, 128], P('clips', None, 'slab')
- video_grad: bfloat16 [64, 6, 16, 16, 256], P('clips', None, 'slab')
- kernel_grad: float32 [256, 3456], P('clips', 'slab')
- gain_grad: float32 [128], replicated
- bias_grad: float32 [128], replicated
Inputs may be any that keep to these rules, and one draw needn't show every extreme that they name: `clip_blocks`: the blocks of all clips add up to 4 times the number of devices along clips, so every device receives exactly 4 blocks; some clip has 3 blocks. `deal_order`: a permutation of the devices along clips.
All inputs are finite; a program needn't handle non-finite values.
Results may differ from a plain program's by a relative error of at most 0.0049.
Values may be sent and summed in bfloat16 or wider, within the bound.
A program may use at most 64 MiB of HBM per device.

v0:
```python
import jax
import jax.numpy as jnp
from jax import lax
from jax.sharding import PartitionSpec as P

GROUPS = 16
TAPS = 27
FB = 2
BMAX = 3


def extended(array, sides, width):
    for axis, dim in sides:
        size, length = (lax.axis_size(axis), array.shape[dim])
        up = [(i, (i + 1) % size) for i in range(size - 1)]
        down = [(j, i) for i, j in up]
        last = lax.slice_in_dim(array, length - width, length, axis=dim)
        initial = lax.slice_in_dim(array, 0, width, axis=dim)
        before = lax.ppermute(last, axis, up)
        after = lax.ppermute(initial, axis, down)
        array = jnp.concatenate([before, array, after], axis=dim)
    return array


def body(video, clip_blocks, deal_order, kernel, gain, bias, cotangent):
    clip_devs = lax.axis_size("clips")
    slab_devs = lax.axis_size("slab")
    own_index = lax.axis_index("clips")
    held_clips, frame_count, row_count, column_count, in_channels = video.shape
    slot_count = cotangent.shape[0]
    out_channels = gain.shape[0]
    all_clips = clip_blocks.shape[0]
    per_group = out_channels // GROUPS
    capacity = -(-(held_clips * BMAX) // clip_devs)
    block_ends = jnp.cumsum(clip_blocks)
    block_starts = block_ends - clip_blocks
    device_ids = jnp.arange(clip_devs, dtype=jnp.int32)
    deal_slot = jnp.sum(
        jnp.where(deal_order[:, None] == device_ids[None, :], device_ids[:, None], 0), axis=0
    )
    first_clip = own_index * held_clips
    own_start = block_starts[first_clip]
    own_end = block_ends[first_clip + held_clips - 1]
    dest_rank = jnp.repeat(device_ids, capacity)
    turn_index = jnp.tile(jnp.arange(capacity, dtype=jnp.int32), clip_devs)
    slot_blocks = jnp.arange(slot_count, dtype=jnp.int32) * clip_devs + deal_slot[own_index]

    def clip_index(block_id):
        return jnp.sum((block_ends <= block_id[..., None]).astype(jnp.int32), axis=-1)

    full_kernel = lax.all_gather(kernel, "slab", axis=1, tiled=True)
    full_kernel = lax.all_gather(full_kernel, "clips", axis=0, tiled=True)
    kernel_taps = full_kernel.reshape(in_channels, out_channels, TAPS).transpose(2, 0, 1)

    def group_sums(values):
        return jnp.sum(values.reshape(values.shape[:4] + (GROUPS, per_group)), axis=(1, 2, 3, 5))

    def spread(stat):
        return stat[:, None, None, None, :, None]

    cells_clip = FB * row_count * slab_devs * column_count * per_group
    context_video = jnp.pad(video, ((0, 0), (2, 0), (0, 0), (0, 0), (0, 0)))
    highest = lax.Precision.HIGHEST
    first_block = own_start + jnp.mod(deal_slot[dest_rank] - own_start, clip_devs)
    block_id = first_block + turn_index * clip_devs
    is_live = block_id < own_end
    clip_global = jnp.minimum(clip_index(block_id), all_clips - 1)
    clip_local = jnp.clip(clip_global - first_clip, 0, held_clips - 1)
    block_local = jnp.clip(block_id - block_starts[clip_global], 0, BMAX - 1)
    window = FB + 2

    def window_of(clip_pick, block_pick):
        begin = (clip_pick, block_pick * FB, 0, 0, 0)
        sizes = (1, window, row_count, column_count, context_video.shape[-1])
        return lax.dynamic_slice(context_video, begin, sizes)[0]

    pieces = jax.vmap(window_of)(clip_local, block_local)
    pieces = jnp.where(
        is_live[:, None, None, None, None], pieces, jnp.zeros((), context_video.dtype)
    )
    sent = pieces.reshape((clip_devs, capacity) + pieces.shape[1:])
    received = lax.all_to_all(sent, "clips", split_axis=0, concat_axis=0, tiled=True)
    clip_global = clip_index(slot_blocks)
    source_rank = clip_global // held_clips
    turn_of = (slot_blocks - block_starts[source_rank * held_clips]) // clip_devs
    flat_rows = received.reshape((clip_devs * capacity,) + received.shape[2:])
    input_slots = flat_rows[source_rank * capacity + turn_of]
    rimmed = extended(input_slots, (("slab", 2),), 1)
    padded = jnp.pad(rimmed, ((0, 0), (0, 0), (0, 0), (1, 1), (0, 0)))
    forward_outputs = input_slots.shape[1] - 2
    totals = jnp.zeros(
        (input_slots.shape[0] * forward_outputs * row_count * column_count, out_channels),
        jnp.float32,
    )
    for forward_step_a in range(3):
        for forward_step_b in range(3):
            for forward_step_c in range(3):
                tap_rows = padded[
                    :,
                    forward_step_a : forward_step_a + forward_outputs,
                    forward_step_b : forward_step_b + row_count,
                    forward_step_c : forward_step_c + column_count,
                    :,
                ].reshape(-1, in_channels)
                totals = totals + jnp.dot(
                    tap_rows,
                    kernel_taps[(forward_step_a * 3 + forward_step_b) * 3 + forward_step_c],
                    preferred_element_type=jnp.float32,
                )
    conv_out = totals.reshape(
        input_slots.shape[0], forward_outputs, row_count, column_count, out_channels
    )
    slot_clip = clip_index(slot_blocks)
    chooser = (slot_clip[:, None] == jnp.arange(all_clips, dtype=jnp.int32)[None, :]).astype(
        jnp.float32
    )
    table_first = jnp.dot(chooser.T, group_sums(conv_out), precision=highest)
    table_second = jnp.dot(chooser.T, group_sums(conv_out * conv_out), precision=highest)
    table_first, table_second = lax.psum((table_first, table_second), ("clips", "slab"))
    counts = (clip_blocks * cells_clip).astype(jnp.float32)
    group_mean = table_first / counts[:, None]
    group_var = table_second / counts[:, None] - group_mean * group_mean
    clip_mean = group_mean
    clip_inv = lax.rsqrt(group_var + 1e-05)
    group_mean = jnp.dot(chooser, clip_mean, precision=highest)
    inv_std = jnp.dot(chooser, clip_inv, precision=highest)
    grouped = conv_out.reshape(conv_out.shape[:4] + (GROUPS, per_group))
    normed = ((grouped - spread(group_mean)) * spread(inv_std)).reshape(conv_out.shape)
    affine = normed * gain + bias
    activations = jax.nn.silu(affine).astype(jnp.bfloat16)
    sigmoid = jax.nn.sigmoid(affine)
    grad_affine = cotangent.astype(jnp.float32) * sigmoid * (1.0 + affine * (1.0 - sigmoid))
    gain_part = jnp.sum(grad_affine * normed, axis=(0, 1, 2, 3))
    bias_part = jnp.sum(grad_affine, axis=(0, 1, 2, 3))
    grad_normed, gain_part, bias_part = (grad_affine * gain, gain_part, bias_part)
    sum_grad = jnp.dot(chooser.T, group_sums(grad_normed), precision=highest)
    sum_cross = jnp.dot(chooser.T, group_sums(grad_normed * normed), precision=highest)
    sum_grad, sum_cross, gain_grad, bias_grad = lax.psum(
        (sum_grad, sum_cross, gain_part, bias_part), ("clips", "slab")
    )
    mean_grad = jnp.dot(chooser, sum_grad / counts[:, None], precision=highest)
    mean_cross = jnp.dot(chooser, sum_cross / counts[:, None], precision=highest)
    grouped = grad_normed.reshape(grad_normed.shape[:4] + (GROUPS, per_group))
    normed_groups = normed.reshape(grouped.shape)
    result = spread(inv_std) * (grouped - spread(mean_grad) - normed_groups * spread(mean_cross))
    grad_conv = result.reshape(grad_normed.shape).astype(jnp.bfloat16)
    range_start = block_starts[dest_rank * held_clips]
    range_end = block_ends[dest_rank * held_clips + held_clips - 1]
    first_block = range_start + jnp.mod(deal_slot[own_index] - range_start, clip_devs)
    block_id = first_block + turn_index * clip_devs
    is_live = block_id < range_end
    slot_index = jnp.clip(block_id // clip_devs, 0, slot_count - 1)
    pieces = jnp.where(
        is_live[:, None, None, None, None], grad_conv[slot_index], jnp.zeros((), grad_conv.dtype)
    )
    returned = lax.all_to_all(
        pieces.reshape((clip_devs, capacity) + pieces.shape[1:]),
        "clips",
        split_axis=0,
        concat_axis=0,
        tiled=True,
    )
    clip_global = first_clip + jnp.arange(held_clips, dtype=jnp.int32)[:, None]
    block_range = jnp.arange(BMAX, dtype=jnp.int32)[None, :]
    block_id = block_starts[clip_global] + block_range
    is_live = block_range < clip_blocks[clip_global]
    source_rank = deal_order[jnp.mod(block_id, clip_devs)]
    turn_of = (block_id - own_start) // clip_devs
    row_index = jnp.where(is_live, source_rank * capacity + turn_of, 0)
    flat_rows = returned.reshape((clip_devs * capacity,) + returned.shape[2:])
    pieces = jnp.where(
        is_live[:, :, None, None, None, None], flat_rows[row_index], jnp.zeros((), returned.dtype)
    )
    grad_clip = pieces.reshape((held_clips, frame_count) + pieces.shape[3:])
    rimmed_grad = extended(grad_clip, (("slab", 2),), 1)
    grad_padded = jnp.pad(rimmed_grad, ((0, 0), (0, 2), (0, 0), (1, 1), (0, 0)))
    totals = jnp.zeros(
        (held_clips * frame_count * row_count * column_count, in_channels), jnp.float32
    )
    for step_a in range(3):
        for step_b in range(3):
            for step_c in range(3):
                moved = grad_padded[
                    :,
                    2 - step_a : 2 - step_a + frame_count,
                    2 - step_b : 2 - step_b + row_count,
                    2 - step_c : 2 - step_c + column_count,
                    :,
                ].reshape(-1, out_channels)
                totals = totals + lax.dot_general(
                    moved,
                    kernel_taps[(step_a * 3 + step_b) * 3 + step_c],
                    (((1,), (1,)), ((), ())),
                    preferred_element_type=jnp.float32,
                )
    video_grad = totals.reshape(video.shape).astype(jnp.bfloat16)
    outputs = grad_conv.shape[1]
    grad_flat = grad_conv.reshape(-1, out_channels)
    take_count = in_channels // clip_devs * lax.axis_size("clips")
    tap_parts = []
    for step_a in range(3):
        for step_b in range(3):
            for step_c in range(3):
                tap_rows = padded[
                    :,
                    step_a : step_a + outputs,
                    step_b : step_b + row_count,
                    step_c : step_c + column_count,
                    :,
                ].reshape(-1, take_count)
                tap_parts.append(
                    lax.dot_general(
                        tap_rows,
                        grad_flat,
                        (((0,), (0,)), ((), ())),
                        preferred_element_type=jnp.float32,
                    )
                )
    partial_grad = lax.psum_scatter(
        jnp.stack(tap_parts, axis=2).reshape(take_count, out_channels * TAPS),
        "clips",
        scatter_dimension=0,
        tiled=True,
    )
    kernel_grad = lax.psum_scatter(partial_grad, "slab", scatter_dimension=1, tiled=True)
    return (activations, video_grad, kernel_grad, gain_grad, bias_grad)


def solution(mesh):
    return jax.shard_map(
        body,
        mesh=mesh,
        in_specs=(
            P("clips", None, "slab", None, None),
            P(),
            P(),
            P("clips", "slab"),
            P(),
            P(),
            P("clips", None, "slab", None, None),
        ),
        out_specs=(
            P("clips", None, "slab", None, None),
            P("clips", None, "slab", None, None),
            P("clips", "slab"),
            P(),
            P(),
        ),
        check_vma=False,
    )
```

profile of v0, /device:TPU:2, one launch (start us, length us, event | category | flops | bytes accessed | tf_op | source)
XLA Modules:
  0.0 642.9 jit_solution(1696978957917538280)
XLA Ops:
  9.0 1.2 multiply_convert_fusion.2
  12.8 1.3 broadcast_compare_fusion
  16.4 1.1 fusion.36
  17.6 9.5 %all-to-all-start = ((bf16[32,1,4,1,16,256]{5,4,2,3,1,0:T(8,128)(2,1)}), bf16[32,1,4,1,16,256]{5,4,2,3,1,0:T(8,128)(2,1)S(1)}, u32[]{:S(2)}, u32[]{:S(2)}) async-start(bf16[32,1,4,1,16,256]{5,4,2,3,1,0:T(8,128)(2,1)} %fusion.36), calls=%async_computation | async-start | bytes 2097152 | tf_op jit(solution)/shard_map/all_to_all | solution.py:82
  27.1 33.9 %all-gather = bf16[16,216,8]{1,2,0:T(8,128)(2,1)S(1)} all-gather(bf16[1,216,8]{1,2,0:T(8,128)(2,1)S(1)} %bitcast.755), channel_id=1, replica_groups=mesh['clips'=32,'slab'=16] {'slab'}, dimensions={0}, use_global_device_ids=true | all-gather | bytes 58752 | tf_op jit(solution)/shard_map/all_gather | solution.py:51
  69.1 1.3 dynamic-slice.1
  73.7 1.3 collective-permute-start.1
  75.0 4.6 collective-permute-start
  80.5 1.5 collective-permute-done
  84.7 31.1 %all-gather.3.cloned.1.call-done = bf16[256,3456]{1,0:T(8,128)(2,1)} async-done(((bf16[8,3456]{1,0:T(8,128)(2,1)}), bf16[256,3456]{1,0:T(8,128)(2,1)}) %all-gather.3.cloned.1.call-update) | async-done | bytes 1769488 | tf_op jit(solution)/shard_map/all_gather | solution.py:52
  115.8 3.9 copy.95
  119.6 2.6 reshape.1229
  122.2 3.5 fusion.224
  125.7 1.8 fusion.225
  127.5 1.1 copy.122
  128.6 1.0 copy.116
  129.7 1.0 copy.113
  131.0 1.0 copy.96
  132.0 1.0 copy.97
  133.1 1.0 copy.98
  134.1 1.0 copy.99
  135.1 1.0 copy.100
  136.2 1.0 copy.101
  137.2 1.0 copy.102
  138.3 1.0 copy.103
  139.3 1.0 copy.105
  140.3 1.0 copy.106
  141.4 1.0 copy.108
  142.4 1.0 copy.109
  143.4 1.0 copy.110
  144.6 1.0 copy.112
  154.0 1.0 convolution_add_fusion.41
  157.0 1.0 fusion.35
  158.0 1.0 convolution_add_fusion.37
  164.0 1.0 fusion.33
  166.0 1.0 fusion.32
  171.3 104.3 %all-reduce.6 = (f32[64,16]{0,1:T(8,128)S(1)}, f32[64,16]{0,1:T(8,128)S(1)}) all-reduce(f32[64,16]{0,1:T(8,128)S(1)} %fusion.160, f32[64,16]{0,1:T(8,128)S(1)} %fusion.161), channel_id=1, replica_groups=mesh['clips'=32,'slab'=16] {'clips','slab'}, use_global_device_ids=true, to_apply=%region_7.8 | all-reduce | flops 2048 | bytes 16384 | tf_op jit(solution)/shard_map/psum | solution.py:119
  277.8 100.7 %all-reduce.5 = (f32[64,16]{0,1:T(8,128)S(1)}, f32[64,16]{0,1:T(8,128)S(1)}, f32[128]{0:T(128)}, f32[128]{0:T(128)}) all-reduce(f32[64,16]{0,1:T(8,128)S(1)} %fusion.158, f32[64,16]{0,1:T(8,128)S(1)} %fusion.159, f32[128]{0:T(128)S(1)} %get-tuple-element.25, ...), channel_id=1, replica_groups=mesh['clips'=32,'slab'=16] {'clips','slab'}, use_global_device_ids=true, to_apply=%region_13.14 | all-reduce | flops 2304 | bytes 18432 | tf_op jit(solution)/shard_map/psum | solution.py:138
  381.6 5.0 all-to-all-start.1
  409.2 6.0 copy.126
  415.3 4.9 reshape.1311
  420.9 1.3 collective-permute-start.3
  422.2 4.5 collective-permute-start.2
  426.9 1.6 collective-permute-done.2
  433.5 124.2 %all-reduce.9.cloned.1.call-done = f32[256,3456]{0,1:T(8,128)} async-done(((f32[256,3456]{0,1:T(8,128)}), f32[256,3456]{0,1:T(8,128)}) %all-reduce.9.cloned.1.call-update) | async-done | bytes 3538960
  557.7 3.2 constant_dynamic-slice_fusion
  561.8 73.0 %reduce-scatter.5.cloned.1.call-done = f32[8,216]{0,1:T(8,128)} async-done(((f32[8,3456]{0,1:T(8,128)}), f32[8,216]{0,1:T(8,128)}) %reduce-scatter.5.cloned.1.call-update) | async-done | bytes 6928
  634.8 1.6 copy.128
  (231 shorter events, 76.2 us)
Async XLA Ops:
  14.2 12.8 %copy-start.15 = (bf16[8,216]{1,0:T(8,128)(2,1)S(1)}, bf16[8,216]{1,0:T(8,128)(2,1)}, u32[]{:S(2)}) copy-start(bf16[8,216]{1,0:T(8,128)(2,1)} %param.10) | copy-start | bytes 10372
  15.7 46.8 %copy-start.1 = (s32[64]{0:T(128)S(1)}, s32[64]{0:T(128)}, u32[]{:S(2)}) copy-start(s32[64]{0:T(128)} %param.8) | copy-start | bytes 772
  15.7 48.2 %copy-start = (s32[32]{0:T(128)S(1)}, s32[32]{0:T(128)}, u32[]{:S(2)}) copy-start(s32[32]{0:T(128)} %param.9) | copy-start | bytes 388
  17.6 55.5 %all-to-all-start = ((bf16[32,1,4,1,16,256]{5,4,2,3,1,0:T(8,128)(2,1)}), bf16[32,1,4,1,16,256]{5,4,2,3,1,0:T(8,128)(2,1)S(1)}, u32[]{:S(2)}, u32[]{:S(2)}) async-start(bf16[32,1,4,1,16,256]{5,4,2,3,1,0:T(8,128)(2,1)} %fusion.36), calls=%async_computation | async-start | bytes 2097152 | tf_op jit(solution)/shard_map/all_to_all | solution.py:82
  27.0 88.8 %all-gather.3.cloned.1.call-start = ((), (), s32[]{:S(2)}) async-start(), calls=%async_computation.3 | async-start | bytes 1824768 | tf_op jit(solution)/shard_map/all_gather | solution.py:52
  65.5 8.2 %copy-start.20 = (s32[4]{0:T(128)}, s32[4]{0:T(128)S(1)}, u32[]{:S(2)}) copy-start(s32[4]{0:T(128)S(1)} %convert_reduce_fusion.1) | copy-start | bytes 52
  73.7 6.9 %collective-permute-start.1 = (bf16[4,4,1,16,256]{4,3,1,0,2:T(8,128)(2,1)S(1)}, bf16[4,4,1,16,256]{4,3,1,0,2:T(8,128)(2,1)S(1)}, u32[]{:S(2)}, u32[]{:S(2)}) collective-permute-start(bf16[4,4,1,16,256]{4,3,1,0,2:T(8,128)(2,1)S(1)} %bitcast.688), channel_id=1, source_target_pairs={{1,0},{2,1},{3,2},{4,3},{5,4},{6,5},{7,6},{8,7},{9,8},{10,9},{11,1... | collective-permute-start | bytes 393224 | tf_op jit(solution)/shard_map/ppermute | solution.py:20
  75.0 7.1 %collective-permute-start = (bf16[4,4,1,16,256]{4,3,1,0,2:T(8,128)(2,1)S(1)}, bf16[4,4,1,16,256]{4,3,1,0,2:T(8,128)(2,1)S(1)}, u32[]{:S(2)}, u32[]{:S(2)}) collective-permute-start(bf16[4,4,1,16,256]{4,3,1,0,2:T(8,128)(2,1)S(1)} %bitcast.689), channel_id=1, source_target_pairs={{0,1},{1,2},{2,3},{3,4},{4,5},{5,6},{6,7},{7,8},{8,9},{9,10},{10,1... | collective-permute-start | bytes 393224 | tf_op jit(solution)/shard_map/ppermute | solution.py:19
  127.5 17.0 %copy-start.8 = (bf16[1,256,128]{1,0,2:T(2,128)(2,1)S(1)}, bf16[1,256,128]{1,0,2:T(2,128)(2,1)}, u32[]{:S(2)}) copy-start(bf16[1,256,128]{1,0,2:T(2,128)(2,1)} %get-tuple-element.49) | copy-start | bytes 196612
  127.5 18.2 %copy-start.7 = (bf16[1,256,128]{1,0,2:T(2,128)(2,1)S(1)}, bf16[1,256,128]{1,0,2:T(2,128)(2,1)}, u32[]{:S(2)}) copy-start(bf16[1,256,128]{1,0,2:T(2,128)(2,1)} %get-tuple-element.46) | copy-start | bytes 196612
  127.5 18.4 %copy-start.6 = (bf16[1,256,128]{1,0,2:T(2,128)(2,1)S(1)}, bf16[1,256,128]{1,0,2:T(2,128)(2,1)}, u32[]{:S(2)}) copy-start(bf16[1,256,128]{1,0,2:T(2,128)(2,1)} %get-tuple-element.45) | copy-start | bytes 196612
  127.5 18.5 %copy-start.5 = (bf16[1,256,128]{1,0,2:T(2,128)(2,1)S(1)}, bf16[1,256,128]{1,0,2:T(2,128)(2,1)}, u32[]{:S(2)}) copy-start(bf16[1,256,128]{1,0,2:T(2,128)(2,1)} %get-tuple-element.43) | copy-start | bytes 196612
  127.5 18.6 %copy-start.4 = (bf16[1,256,128]{1,0,2:T(2,128)(2,1)S(1)}, bf16[1,256,128]{1,0,2:T(2,128)(2,1)}, u32[]{:S(2)}) copy-start(bf16[1,256,128]{1,0,2:T(2,128)(2,1)} %get-tuple-element.42) | copy-start | bytes 196612
  127.5 18.8 %copy-start.3 = (bf16[1,256,128]{1,0,2:T(2,128)(2,1)S(1)}, bf16[1,256,128]{1,0,2:T(2,128)(2,1)}, u32[]{:S(2)}) copy-start(bf16[1,256,128]{1,0,2:T(2,128)(2,1)} %get-tuple-element.41) | copy-start | bytes 196612
  127.5 18.9 %copy-start.2 = (bf16[1,256,128]{1,0,2:T(2,128)(2,1)S(1)}, bf16[1,256,128]{1,0,2:T(2,128)(2,1)}, u32[]{:S(2)}) copy-start(bf16[1,256,128]{1,0,2:T(2,128)(2,1)} %get-tuple-element.40) | copy-start | bytes 196612
  127.5 23.2 %copy-start.9 = (bf16[4,2,1,16,256]{4,3,1,0,2:T(8,128)(2,1)S(1)}, bf16[4,2,1,16,256]{4,3,1,0,2:T(8,128)(2,1)}, u32[]{:S(2)}) copy-start(bf16[4,2,1,16,256]{4,3,1,0,2:T(8,128)(2,1)} %get-tuple-element.76) | copy-start | bytes 196612
  145.8 21.2 %copy-start.12 = (bf16[4,2,1,16,256]{4,3,1,0,2:T(8,128)(2,1)S(1)}, bf16[4,2,1,16,256]{4,3,1,0,2:T(8,128)(2,1)}, u32[]{:S(2)}) copy-start(bf16[4,2,1,16,256]{4,3,1,0,2:T(8,128)(2,1)} %get-tuple-element.67) | copy-start | bytes 196612
  146.1 22.0 %copy-start.11 = (bf16[4,2,1,16,256]{4,3,1,0,2:T(8,128)(2,1)S(1)}, bf16[4,2,1,16,256]{4,3,1,0,2:T(8,128)(2,1)}, u32[]{:S(2)}) copy-start(bf16[4,2,1,16,256]{4,3,1,0,2:T(8,128)(2,1)} %get-tuple-element.66) | copy-start | bytes 196612
  146.3 22.0 %copy-start.10 = (bf16[4,2,1,16,256]{4,3,1,0,2:T(8,128)(2,1)S(1)}, bf16[4,2,1,16,256]{4,3,1,0,2:T(8,128)(2,1)}, u32[]{:S(2)}) copy-start(bf16[4,2,1,16,256]{4,3,1,0,2:T(8,128)(2,1)} %get-tuple-element.65) | copy-start | bytes 196612
  146.6 21.9 %copy-start.13 = (bf16[4,2,1,16,256]{4,3,1,0,2:T(8,128)(2,1)S(1)}, bf16[4,2,1,16,256]{4,3,1,0,2:T(8,128)(2,1)}, u32[]{:S(2)}) copy-start(bf16[4,2,1,16,256]{4,3,1,0,2:T(8,128)(2,1)} %get-tuple-element.107) | copy-start | bytes 196612
  152.0 17.8 %copy-start.21 = (s32[4]{0:T(128)S(1)}, s32[4]{0:T(128)}, u32[]{:S(2)}) copy-start(s32[4]{0:T(128)} %copy-done.20) | copy-start | bytes 52
  157.0 118.6 %copy-start.19 = (f32[64]{0:T(128)S(1)}, f32[64]{0:T(128)}, u32[]{:S(2)}) copy-start(f32[64]{0:T(128)} %get-tuple-element.117) | copy-start | bytes 772
  158.0 118.3 %copy-start.14 = (bf16[4,2,1,16,128]{4,3,2,1,0:T(8,128)(2,1)S(1)}, bf16[4,2,1,16,128]{4,3,2,1,0:T(8,128)(2,1)}, u32[]{:S(2)}) copy-start(bf16[4,2,1,16,128]{4,3,2,1,0:T(8,128)(2,1)} %param.13) | copy-start | bytes 98308
  158.0 118.3 %copy-start.16 = (f32[128]{0:T(128)S(1)}, f32[128]{0:T(128)}, u32[]{:S(2)}) copy-start(f32[128]{0:T(128)} %param.11) | copy-start | bytes 1540
  158.0 118.3 %copy-start.17 = (f32[128]{0:T(128)S(1)}, f32[128]{0:T(128)}, u32[]{:S(2)}) copy-start(f32[128]{0:T(128)} %param.12) | copy-start | bytes 1540
  381.6 38.6 %all-to-all-start.1 = ((bf16[32,1,2,1,16,128]{5,4,2,3,1,0:T(8,128)(2,1)}), bf16[32,1,2,1,16,128]{5,4,2,3,1,0:T(8,128)(2,1)S(1)}, u32[]{:S(2)}, u32[]{:S(2)}) async-start(bf16[32,1,2,1,16,128]{5,4,2,3,1,0:T(8,128)(2,1)} %bitcast_select_fusion.1), calls=%async_computation.1 | async-start | bytes 524288 | tf_op jit(solution)/shard_map/all_to_all | solution.py:156
  386.6 171.2 %all-reduce.9.cloned.1.call-start = ((), (), s32[]{:S(2)}) async-start(), calls=%async_computation.4 | async-start | bytes 7077888
  420.1 0.7 copy-start.18
  420.2 214.6 %reduce-scatter.5.cloned.1.call-start = ((), (), s32[]{:S(2)}) async-start(), calls=%async_computation.5 | async-start | bytes 1880064
  420.9 6.0 collective-permute-start.3
  422.2 6.3 collective-permute-start.2
Sparse Core Ops, SparseCore 0:
  61.9 53.8 all-gather.2
  420.3 137.3 all-reduce.8
  561.1 73.6 reduce-scatter.4
where the time goes:
time: 645 us; the launch traced here: 643 us
  blocking collectives  239 us (37%)
  waiting for transfers between devices  232 us (36%)
  local copies, waits for them, and re-layouts  66.3 us (10%)
  matrix products  52.1 us (8%)
  starting transfers between devices  26.2 us (4%)
  between operations  15.4 us (2%)
  other arithmetic  12.1 us (2%)
    unnamed x5, waiting for transfers between devices  197 us
    psum x1, blocking collectives, body(): lax.psum((table_first, table_second), ('clips', 'slab'))  104 us
    psum x1, blocking collectives, body(): lax.psum((sum_grad, sum_cross, gain_part, bias_part), ('clips', 'slab'))  101 us
    all_gather x1, blocking collectives, body(): full_kernel = lax.all_gather(kernel, 'slab', axis=1, tiled=True)  33.9 us
    all_gather x1, waiting for transfers between devices, body(): full_kernel = lax.all_gather(full_kernel, 'clips', axis=0, tiled=True)  31.1 us
    slice x29, local copies, waits for them, and re-layouts, body(): kernel_taps[(forward_step_a * 3 + forward_step_b) * 3 + forward_step_c]  24.2 us
    dot_general x27, matrix products, body(): lax.dot_general(tap_rows, grad_flat, (((0,), (0,)), ((), ())), preferred_...  23.5 us
    dot_general x27, matrix products, body(): jnp.dot(tap_rows, kernel_taps[(forward_step_a * 3 + forward_step_b) * 3 +...  21.6 us
  transfers between devices with their start and end apart: 9, of which 6 were waited for; matrix products, arithmetic and copies ran while one was open for 9% of the time, Pallas kernels for 0%

commit v1 on v0

--- a/solution.py
+++ b/solution.py
@@ -49,7 +49,9 @@
         return jnp.sum((block_ends <= block_id[..., None]).astype(jnp.int32), axis=-1)
 
     full_kernel = lax.all_gather(kernel, "slab", axis=1, tiled=True)
-    full_kernel = lax.all_gather(full_kernel, "clips", axis=0, tiled=True)
+    full_kernel = jnp.concatenate(
+        lax.all_to_all(jnp.stack([full_kernel] * lax.axis_size("clips")), "clips", 0, 0), axis=0
+    )
     kernel_taps = full_kernel.reshape(in_channels, out_channels, TAPS).transpose(2, 0, 1)
 
     def group_sums(values):

time: 645 us -> 768 us (1.19)
  local copies, waits for them, and re-layouts: 66.3 us -> 218 us
  waiting for transfers between devices: 232 us -> 211 us
  matrix products: 52.1 us -> 41.9 us
    slice x29 -> x2, local copies, waits for them, and re-layouts: 24.2 us -> 161 us  [body(): kernel_taps[(forward_step_a * 3 + forward_step_b) * 3 + forward_step_c]]
    all_gather x1 -> x0, waiting for transfers between devices: 31.1 us -> none  [body(): full_kernel = lax.all_gather(full_kernel, 'clips', axis=0, tiled=True)]
    another operation x0 -> x2, local copies, waits for them, and re-layouts: none -> 22.5 us  [the longest x1 21.2 us: body(): full_kernel.reshape(in_channels, out_channels, TAPS).transpose(2, 0, 1)]
    all_to_all x0 -> x1, waiting for transfers between devices: none -> 11.2 us  [body(): lax.all_to_all(jnp.stack([full_kernel] * lax.axis_size('clips')), 'clips'...]
    dot_general x27, matrix products: 21.6 us -> 11.5 us  [body(): jnp.dot(tap_rows, kernel_taps[(forward_step_a * 3 + forward_step_b) * 3 +...]
    unnamed x5 -> x4, waiting for transfers between devices: 197 us -> 196 us
  transfers between devices with their start and end apart: 9 -> 9, of which waited for: 6 -> 6; matrix products, arithmetic and copies ran while one was open for 9% -> 7% of each run, Pallas kernels for 0% -> 0%
where the time goes in v1:
time: 768 us; the launch traced here: 767 us
  blocking collectives  234 us (30%)
  local copies, waits for them, and re-layouts  218 us (28%)
  waiting for transfers between devices  211 us (27%)
  matrix products  41.9 us (5%)
  starting transfers between devices  33.8 us (4%)
  between operations  15.6 us (2%)
  other arithmetic  12.1 us (2%)
    unnamed x4, waiting for transfers between devices  196 us
    slice x2, local copies, waits for them, and re-layouts, body(): kernel_taps[(forward_step_a * 3 + forward_step_b) * 3 + forward_step_c]  161 us
    psum x1, blocking collectives, body(): lax.psum((sum_grad, sum_cross, gain_part, bias_part), ('clips', 'slab'))  101 us
    psum x1, blocking collectives, body(): lax.psum((table_first, table_second), ('clips', 'slab'))  99.6 us
    all_gather x1, blocking collectives, body(): full_kernel = lax.all_gather(kernel, 'slab', axis=1, tiled=True)  33.9 us
    dot_general x27, matrix products, body(): lax.dot_general(tap_rows, grad_flat, (((0,), (0,)), ((), ())), preferred_...  23.3 us
    another operation x1, local copies, waits for them, and re-layouts, body(): full_kernel.reshape(in_channels, out_channels, TAPS).transpose(2, 0, 1)  21.2 us
  transfers between devices with their start and end apart: 9, of which 6 were waited for; matrix products, arithmetic and copies ran while one was open for 7% of the time, Pallas kernels for 0%

profile of v1, /device:TPU:2, one launch (start us, length us, event | category | flops | bytes accessed | tf_op | source)
XLA Modules:
  0.0 766.7 jit_solution(3550486191258491537)
XLA Ops:
  7.2 0.9 copy.37
  9.0 1.2 multiply_convert_fusion.2
  12.8 1.3 broadcast_compare_fusion
  16.4 1.1 fusion.36
  17.5 9.5 %all-to-all-start = ((bf16[32,1,4,1,16,256]{5,4,2,3,1,0:T(8,128)(2,1)}), bf16[32,1,4,1,16,256]{5,4,2,3,1,0:T(8,128)(2,1)S(1)}, u32[]{:S(2)}, u32[]{:S(2)}) async-start(bf16[32,1,4,1,16,256]{5,4,2,3,1,0:T(8,128)(2,1)} %fusion.36), calls=%async_computation | async-start | bytes 2097152 | tf_op jit(solution)/shard_map/all_to_all | solution.py:84
  29.2 33.9 %all-gather = bf16[16,216,8]{1,2,0:T(8,128)(2,1)S(1)} all-gather(bf16[1,216,8]{1,2,0:T(8,128)(2,1)S(1)} %bitcast.670), channel_id=1, replica_groups=mesh['clips'=32,'slab'=16] {'slab'}, dimensions={0}, use_global_device_ids=true | all-gather | bytes 58752 | tf_op jit(solution)/shard_map/all_gather | solution.py:51
  68.4 1.3 dynamic-slice.1
  71.0 1.3 stack.58
  72.3 7.4 all-to-all-start.1
  81.6 1.3 collective-permute-start.1
  82.9 4.7 collective-permute-start
  89.1 1.2 collective-permute-done
  91.9 1.0 fusion.161
  92.8 11.2 %all-to-all-done.1 = bf16[32,8,3456]{2,1,0:T(8,128)(2,1)S(1)} async-done(((bf16[32,8,3456]{2,1,0:T(8,128)(2,1)}), bf16[32,8,3456]{2,1,0:T(8,128)(2,1)S(1)}, u32[]{:S(2)}, u32[]{:S(2)}) %all-to-all-start.1) | async-done | bytes 1769504 | tf_op jit(solution)/shard_map/all_to_all | solution.py:53
  104.0 21.2 %reshape_reshape.9 = bf16[256,128,27]{2,1,0:T(8,128)(2,1)} reshape(bf16[32,8,3456]{2,1,0:T(8,128)(2,1)S(1)} %all-to-all-done.1) | data formatting | bytes 3538944 | tf_op jit(solution)/shard_map/reshape;reshape | solution.py:55
  125.2 114.4 %slice_reduce_fusion.1 = (bf16[256,128]{1,0:T(8,128)(2,1)S(1)}, bf16[256,128]{1,0:T(8,128)(2,1)S(1)}, bf16[256,128]{1,0:T(8,128)(2,1)S(1)}, bf16[256,128]{1,0:T(...) fusion(bf16[27,256,128]{0,2,1:T(8,128)(2,1)} %bitcast.600), kind=kLoop, calls=%fused_computation.13 | loop fusion | bytes 2490368 | tf_op jit(solution)/shard_map/slice | solution.py:109
  239.6 46.5 %slice_reduce_fusion.19 = (bf16[256,128]{1,0:T(8,128)(2,1)S(1)}, bf16[256,128]{1,0:T(8,128)(2,1)S(1)}, bf16[256,128]{1,0:T(8,128)(2,1)S(1)}, bf16[256,128]{1,0:T...) fusion(bf16[27,256,128]{0,2,1:T(8,128)(2,1)} %bitcast.601), kind=kLoop, calls=%fused_computation.31 | loop fusion | bytes 1048576 | tf_op jit(solution)/shard_map/slice | solution.py:109
  287.2 1.0 convolution_add_fusion.44
  288.2 1.0 convolution_add_fusion.43
  289.2 1.0 convolution_add_fusion.42
  290.2 1.0 convolution_add_fusion.41
  291.2 1.0 convolution_add_fusion.40
  292.1 1.0 convolution_add_fusion.39
  293.2 1.0 fusion.35
  294.2 1.0 convolution_add_fusion.37
  295.2 1.0 fusion.34
  300.8 99.6 %all-reduce.6 = (f32[64,16]{0,1:T(8,128)S(1)}, f32[64,16]{0,1:T(8,128)S(1)}) all-reduce(f32[64,16]{0,1:T(8,128)S(1)} %fusion.97, f32[64,16]{0,1:T(8,128)S(1)} %fusion.98), channel_id=1, replica_groups=mesh['clips'=32,'slab'=16] {'clips','slab'}, use_global_device_ids=true, to_apply=%region_7.8 | all-reduce | flops 2048 | bytes 16384 | tf_op jit(solution)/shard_map/psum | solution.py:121
  402.7 100.8 %all-reduce.5 = (f32[64,16]{0,1:T(8,128)S(1)}, f32[64,16]{0,1:T(8,128)S(1)}, f32[128]{0:T(128)}, f32[128]{0:T(128)}) all-reduce(f32[64,16]{0,1:T(8,128)S(1)} %fusion.95, f32[64,16]{0,1:T(8,128)S(1)} %fusion.96, f32[128]{0:T(128)S(1)} %get-tuple-element.52, ...), channel_id=1, replica_groups=mesh['clips'=32,'slab'=16] {'clips','slab'}, use_global_device_ids=true, to_apply=%region_13.14 | all-reduce | flops 2304 | bytes 18432 | tf_op jit(solution)/shard_map/psum | solution.py:140
  506.6 5.0 all-to-all-start.2
  513.3 0.9 fusion.27
  514.2 0.9 fusion.26
  516.8 0.9 fusion.23
  518.5 0.9 fusion.21
  519.3 0.9 fusion.20
  520.2 0.9 fusion.19
  521.1 0.9 fusion.18
  522.0 0.9 fusion.17
  522.8 0.9 fusion.16
  530.6 0.9 fusion.7
  534.1 6.0 copy.43
  540.1 4.9 reshape.1309
  545.7 1.3 collective-permute-start.3
  547.0 4.5 collective-permute-start.2
  551.7 1.6 collective-permute-done.2
  558.3 122.9 %all-reduce.9.cloned.1.call-done = f32[256,3456]{0,1:T(8,128)} async-done(((f32[256,3456]{0,1:T(8,128)}), f32[256,3456]{0,1:T(8,128)}) %all-reduce.9.cloned.1.call-update) | async-done | bytes 3538960
  681.3 3.2 constant_dynamic-slice_fusion
  685.3 73.0 %reduce-scatter.5.cloned.1.call-done = f32[8,216]{0,1:T(8,128)} async-done(((f32[8,3456]{0,1:T(8,128)}), f32[8,216]{0,1:T(8,128)}) %reduce-scatter.5.cloned.1.call-update) | async-done | bytes 6928
  758.3 1.6 copy.45
  (209 shorter events, 49.8 us)
Async XLA Ops:
  15.6 13.6 %copy-start.18 = (bf16[8,216]{1,0:T(8,128)(2,1)S(1)}, bf16[8,216]{1,0:T(8,128)(2,1)}, u32[]{:S(2)}) copy-start(bf16[8,216]{1,0:T(8,128)(2,1)} %param.10) | copy-start | bytes 10372
  15.7 47.5 %copy-start.1 = (s32[64]{0:T(128)S(1)}, s32[64]{0:T(128)}, u32[]{:S(2)}) copy-start(s32[64]{0:T(128)} %param.8) | copy-start | bytes 772
  16.4 49.7 %copy-start = (s32[32]{0:T(128)S(1)}, s32[32]{0:T(128)}, u32[]{:S(2)}) copy-start(s32[32]{0:T(128)} %param.9) | copy-start | bytes 388
  17.5 53.4 %all-to-all-start = ((bf16[32,1,4,1,16,256]{5,4,2,3,1,0:T(8,128)(2,1)}), bf16[32,1,4,1,16,256]{5,4,2,3,1,0:T(8,128)(2,1)S(1)}, u32[]{:S(2)}, u32[]{:S(2)}) async-start(bf16[32,1,4,1,16,256]{5,4,2,3,1,0:T(8,128)(2,1)} %fusion.36), calls=%async_computation | async-start | bytes 2097152 | tf_op jit(solution)/shard_map/all_to_all | solution.py:84
  28.5 43.9 %copy-start.23 = (s32[4]{0:T(128)}, s32[4]{0:T(128)S(1)}, u32[]{:S(2)}) copy-start(s32[4]{0:T(128)S(1)} %convert_reduce_fusion.1) | copy-start | bytes 52
  72.3 31.7 %all-to-all-start.1 = ((bf16[32,8,3456]{2,1,0:T(8,128)(2,1)}), bf16[32,8,3456]{2,1,0:T(8,128)(2,1)S(1)}, u32[]{:S(2)}, u32[]{:S(2)}) async-start(bf16[32,8,3456]{2,1,0:T(8,128)(2,1)} %stack.58), calls=%async_computation.1 | async-start | bytes 3538944 | tf_op jit(solution)/shard_map/all_to_all | solution.py:53
  81.6 7.4 collective-permute-start.1
  82.9 7.3 collective-permute-start
  239.6 46.6 %copy-start.4 = (bf16[4,2,1,16,256]{4,3,1,0,2:T(8,128)(2,1)S(1)}, bf16[4,2,1,16,256]{4,3,1,0,2:T(8,128)(2,1)}, u32[]{:S(2)}) copy-start(bf16[4,2,1,16,256]{4,3,1,0,2:T(8,128)(2,1)} %get-tuple-element.82) | copy-start | bytes 196612
  239.6 46.8 %copy-start.3 = (bf16[4,2,1,16,256]{4,3,1,0,2:T(8,128)(2,1)S(1)}, bf16[4,2,1,16,256]{4,3,1,0,2:T(8,128)(2,1)}, u32[]{:S(2)}) copy-start(bf16[4,2,1,16,256]{4,3,1,0,2:T(8,128)(2,1)} %get-tuple-element.68) | copy-start | bytes 196612
  239.6 46.9 %copy-start.2 = (bf16[4,2,1,16,256]{4,3,1,0,2:T(8,128)(2,1)S(1)}, bf16[4,2,1,16,256]{4,3,1,0,2:T(8,128)(2,1)}, u32[]{:S(2)}) copy-start(bf16[4,2,1,16,256]{4,3,1,0,2:T(8,128)(2,1)} %get-tuple-element.70) | copy-start | bytes 196612
  286.1 10.1 %copy-start.13 = (bf16[4,2,1,16,256]{4,3,1,0,2:T(8,128)(2,1)S(1)}, bf16[4,2,1,16,256]{4,3,1,0,2:T(8,128)(2,1)}, u32[]{:S(2)}) copy-start(bf16[4,2,1,16,256]{4,3,1,0,2:T(8,128)(2,1)} %get-tuple-element.73) | copy-start | bytes 196612
  286.1 10.2 %copy-start.16 = (bf16[4,2,1,16,256]{4,3,1,0,2:T(8,128)(2,1)S(1)}, bf16[4,2,1,16,256]{4,3,1,0,2:T(8,128)(2,1)}, u32[]{:S(2)}) copy-start(bf16[4,2,1,16,256]{4,3,1,0,2:T(8,128)(2,1)} %get-tuple-element.111) | copy-start | bytes 196612
  286.1 10.4 %copy-start.12 = (bf16[4,2,1,16,256]{4,3,1,0,2:T(8,128)(2,1)S(1)}, bf16[4,2,1,16,256]{4,3,1,0,2:T(8,128)(2,1)}, u32[]{:S(2)}) copy-start(bf16[4,2,1,16,256]{4,3,1,0,2:T(8,128)(2,1)} %get-tuple-element.72) | copy-start | bytes 196612
  286.1 10.5 %copy-start.11 = (bf16[4,2,1,16,256]{4,3,1,0,2:T(8,128)(2,1)S(1)}, bf16[4,2,1,16,256]{4,3,1,0,2:T(8,128)(2,1)}, u32[]{:S(2)}) copy-start(bf16[4,2,1,16,256]{4,3,1,0,2:T(8,128)(2,1)} %get-tuple-element.71) | copy-start | bytes 196612
  286.1 10.7 %copy-start.7 = (bf16[4,2,1,16,256]{4,3,1,0,2:T(8,128)(2,1)S(1)}, bf16[4,2,1,16,256]{4,3,1,0,2:T(8,128)(2,1)}, u32[]{:S(2)}) copy-start(bf16[4,2,1,16,256]{4,3,1,0,2:T(8,128)(2,1)} %get-tuple-element.108) | copy-start | bytes 196612
  286.2 10.8 %copy-start.10 = (bf16[4,2,1,16,256]{4,3,1,0,2:T(8,128)(2,1)S(1)}, bf16[4,2,1,16,256]{4,3,1,0,2:T(8,128)(2,1)}, u32[]{:S(2)}) copy-start(bf16[4,2,1,16,256]{4,3,1,0,2:T(8,128)(2,1)} %get-tuple-element.69) | copy-start | bytes 196612
  286.2 11.0 %copy-start.5 = (bf16[4,2,1,16,256]{4,3,1,0,2:T(8,128)(2,1)S(1)}, bf16[4,2,1,16,256]{4,3,1,0,2:T(8,128)(2,1)}, u32[]{:S(2)}) copy-start(bf16[4,2,1,16,256]{4,3,1,0,2:T(8,128)(2,1)} %get-tuple-element.113) | copy-start | bytes 196612
  286.2 11.1 %copy-start.9 = (bf16[4,2,1,16,256]{4,3,1,0,2:T(8,128)(2,1)S(1)}, bf16[4,2,1,16,256]{4,3,1,0,2:T(8,128)(2,1)}, u32[]{:S(2)}) copy-start(bf16[4,2,1,16,256]{4,3,1,0,2:T(8,128)(2,1)} %get-tuple-element.67) | copy-start | bytes 196612
  286.2 11.3 %copy-start.14 = (bf16[4,2,1,16,256]{4,3,1,0,2:T(8,128)(2,1)S(1)}, bf16[4,2,1,16,256]{4,3,1,0,2:T(8,128)(2,1)}, u32[]{:S(2)}) copy-start(bf16[4,2,1,16,256]{4,3,1,0,2:T(8,128)(2,1)} %get-tuple-element.110) | copy-start | bytes 196612
  286.2 11.4 %copy-start.8 = (bf16[4,2,1,16,256]{4,3,1,0,2:T(8,128)(2,1)S(1)}, bf16[4,2,1,16,256]{4,3,1,0,2:T(8,128)(2,1)}, u32[]{:S(2)}) copy-start(bf16[4,2,1,16,256]{4,3,1,0,2:T(8,128)(2,1)} %get-tuple-element.66) | copy-start | bytes 196612
  286.2 11.6 %copy-start.6 = (bf16[4,2,1,16,256]{4,3,1,0,2:T(8,128)(2,1)S(1)}, bf16[4,2,1,16,256]{4,3,1,0,2:T(8,128)(2,1)}, u32[]{:S(2)}) copy-start(bf16[4,2,1,16,256]{4,3,1,0,2:T(8,128)(2,1)} %get-tuple-element.65) | copy-start | bytes 196612
  286.2 11.7 %copy-start.15 = (bf16[4,2,1,16,256]{4,3,1,0,2:T(8,128)(2,1)S(1)}, bf16[4,2,1,16,256]{4,3,1,0,2:T(8,128)(2,1)}, u32[]{:S(2)}) copy-start(bf16[4,2,1,16,256]{4,3,1,0,2:T(8,128)(2,1)} %get-tuple-element.107) | copy-start | bytes 196612
  288.2 11.1 %copy-start.24 = (s32[4]{0:T(128)S(1)}, s32[4]{0:T(128)}, u32[]{:S(2)}) copy-start(s32[4]{0:T(128)} %copy-done.23) | copy-start | bytes 52
  293.1 107.3 %copy-start.22 = (f32[64]{0:T(128)S(1)}, f32[64]{0:T(128)}, u32[]{:S(2)}) copy-start(f32[64]{0:T(128)} %get-tuple-element.117) | copy-start | bytes 772
  294.2 107.0 %copy-start.17 = (bf16[4,2,1,16,128]{4,3,2,1,0:T(8,128)(2,1)S(1)}, bf16[4,2,1,16,128]{4,3,2,1,0:T(8,128)(2,1)}, u32[]{:S(2)}) copy-start(bf16[4,2,1,16,128]{4,3,2,1,0:T(8,128)(2,1)} %param.13) | copy-start | bytes 98308
  294.2 107.0 %copy-start.19 = (f32[128]{0:T(128)S(1)}, f32[128]{0:T(128)}, u32[]{:S(2)}) copy-start(f32[128]{0:T(128)} %param.11) | copy-start | bytes 1540
  294.2 107.0 %copy-start.20 = (f32[128]{0:T(128)S(1)}, f32[128]{0:T(128)}, u32[]{:S(2)}) copy-start(f32[128]{0:T(128)} %param.12) | copy-start | bytes 1540
  506.6 38.5 %all-to-all-start.2 = ((bf16[32,1,2,1,16,128]{5,4,2,3,1,0:T(8,128)(2,1)}), bf16[32,1,2,1,16,128]{5,4,2,3,1,0:T(8,128)(2,1)S(1)}, u32[]{:S(2)}, u32[]{:S(2)}) async-start(bf16[32,1,2,1,16,128]{5,4,2,3,1,0:T(8,128)(2,1)} %bitcast_select_fusion.1), calls=%async_computation.2 | async-start | bytes 524288 | tf_op jit(solution)/shard_map/all_to_all | solution.py:158
  511.5 169.7 %all-reduce.9.cloned.1.call-start = ((), (), s32[]{:S(2)}) async-start(), calls=%async_computation.4 | async-start | bytes 7077888
  544.9 0.7 copy-start.21
  545.0 213.4 %reduce-scatter.5.cloned.1.call-start = ((), (), s32[]{:S(2)}) async-start(), calls=%async_computation.5 | async-start | bytes 1880064
  545.7 6.0 collective-permute-start.3
  547.0 6.3 collective-permute-start.2
Sparse Core Ops, SparseCore 0:
  545.1 136.1 all-reduce.8
  684.6 73.6 reduce-scatter.4
